TPU v7x, 256 devices: a whole 4x4x8 slice. The times are simulated.
256 devices in a mesh: layer: 2 (over core), row: 8 (over z_hi, y), col: 16 (over x, z_lo).
Axes of the slice: x: 4, y: 4, z: 8 (z_hi: 2, z_lo: 4; z = z_hi * 4 + z_lo), core: 2. Of those that a mesh axis runs over, the one named last changes fastest.
Arguments:
- amplitudes: bfloat16 [512, 128, 128], P(('row', 'col')), may hold values from -6 to 6
- integrals: bfloat16 [32768, 128, 128], P(('layer', 'row', 'col')), may hold values from -0.1875 to 0.1875
- amp_index: int32 [4096, 48], P(('layer', 'row', 'col')), may hold values from 0 to 31
- left_index: int32 [4096, 48], P(('layer', 'row', 'col')), may hold values from 0 to 127, as said below
- right_index: int32 [4096, 48], P(('layer', 'row', 'col')), may hold values from 0 to 127, as said below
- dest_col: int32 [2048, 1], P(('row', 'col')), may hold values from 0 to 15; in each aligned block of 16 rows (0 to 15, 16 to 31, ...) at most 2 rows name the same one
- owner_slot: int32 [2048], P(('row', 'col')), may hold values from 0 to 7
Outputs:
- ladder: float32 [1024, 128, 128], P(('row', 'col'))
Inputs may be any that keep to these rules, and one draw needn't show every extreme that they name: `dest_col`: among the 16 result tiles of one index of row and col, no owner column appears more than 2 times, and some column appears exactly 2 times. A term's amplitude tile is number amp_index among the tiles of the devices with the same col index, counted row by row. A term's left and right integral tiles belong to one auxiliary function: left_index // 2 == right_index // 2. right_index // 2 == left_index // 2 for every term.
All inputs are finite; a program needn't handle non-finite values.
Results may differ from a plain program's by a relative error of at most 0.0029.
Values may be sent and summed in bfloat16 or wider, within the bound.
A program may use at most 64 MiB of HBM per device.

v0:
```python
import jax
import jax.numpy as jnp
from jax import lax
from jax.sharding import PartitionSpec as P

OWN = 8
CAP = 2


def select_tiles(stack_flat, picks, count, tile_edge):
    onehot = (picks[:, None] == jnp.arange(count, dtype=jnp.int32)[None, :]).astype(jnp.bfloat16)
    chosen = jnp.dot(onehot, stack_flat, preferred_element_type=jnp.float32).astype(jnp.bfloat16)
    return chosen.reshape(picks.shape[0], tile_edge, tile_edge)


def shards(amplitudes, integrals, amp_index, left_index, right_index, dest_col, owner_slot):
    columns = lax.axis_size("col")
    slot_count = dest_col.shape[0]
    tile_edge = integrals.shape[1]
    gathered = lax.all_gather(amplitudes, "row", axis=0, tiled=True)
    amp_total = gathered.shape[0]
    int_total = integrals.shape[0]
    amp_flat = gathered.reshape(amp_total, tile_edge * tile_edge)
    int_flat = integrals.reshape(int_total, tile_edge * tile_edge)

    def one_slot(operand_list):
        amp_ids, left_ids, right_ids = operand_list
        amp_tiles = select_tiles(amp_flat, amp_ids, amp_total, tile_edge)
        right_tiles = select_tiles(int_flat, right_ids, int_total, tile_edge)
        middle_product = jnp.einsum(
            "tcd,ted->tce", amp_tiles, right_tiles, preferred_element_type=jnp.float32
        ).astype(jnp.bfloat16)
        left_tile_blocks = select_tiles(int_flat, left_ids, int_total, tile_edge)
        return jnp.einsum(
            "dov,dvh->oh", left_tile_blocks, middle_product, preferred_element_type=jnp.float32
        )

    partials = lax.map(one_slot, (amp_index, left_index, right_index))
    target = dest_col[:, 0]
    counter = jnp.arange(slot_count, dtype=jnp.int32)
    earlier = (target[:, None] == target[None, :]) & (counter[None, :] < counter[:, None])
    position_in = jnp.sum(earlier.astype(jnp.int32), axis=1)
    position = target * CAP + position_in
    placing = (position[None, :] == jnp.arange(columns * CAP, dtype=jnp.int32)[:, None]).astype(
        jnp.float32
    )
    buffer = jnp.dot(
        placing,
        partials.reshape(slot_count, tile_edge * tile_edge),
        precision=lax.Precision.HIGHEST,
        preferred_element_type=jnp.float32,
    )
    buffer = buffer.reshape(columns, CAP, tile_edge, tile_edge)
    labels = (
        jnp.full((columns * CAP,), OWN, jnp.int32)
        .at[position]
        .set(owner_slot)
        .reshape(columns, CAP)
    )
    tiles_in, labels_in = (
        lax.all_to_all(buffer, "col", split_axis=0, concat_axis=0, tiled=True),
        lax.all_to_all(labels, "col", split_axis=0, concat_axis=0, tiled=True),
    )
    flattened = tiles_in.reshape(-1, tile_edge * tile_edge)
    owner_mask = (
        labels_in.reshape(-1)[:, None] == jnp.arange(OWN, dtype=jnp.int32)[None, :]
    ).astype(jnp.float32)
    owned_tiles = jnp.dot(
        owner_mask.T, flattened, precision=lax.Precision.HIGHEST, preferred_element_type=jnp.float32
    )
    owned_tiles = lax.psum(owned_tiles, "layer")
    return owned_tiles.reshape(OWN, tile_edge, tile_edge)


def solution(mesh):
    placed = (
        P(("row", "col"), None, None),
        P(("layer", "row", "col"), None, None),
        P(("layer", "row", "col"), None),
        P(("layer", "row", "col"), None),
        P(("layer", "row", "col"), None),
        P(("row", "col"), None),
        P(("row", "col")),
    )
    return jax.shard_map(
        shards, mesh=mesh, in_specs=placed, out_specs=P(("row", "col"), None, None), check_vma=False
    )
```

profile of v0, /device:TPU:1, one launch (start us, length us, event | category | flops | bytes accessed | tf_op | source)
XLA Modules:
  0.0 384.1 jit_solution(10383428219554340299)
XLA Ops:
  10.3 9.0 %all-to-all-start = ((s32[16,1,2]{2,1,0:T(1,128)}), s32[16,1,2]{2,1,0:T(1,128)S(1)}, u32[]{:S(2)}, u32[]{:S(2)}) async-start(s32[16,1,2]{2,1,0:T(1,128)} %bitcast.8), calls=%async_computation | async-start | bytes 16384 | tf_op jit(solution)/shard_map/all_to_all | solution.py:62
  19.3 7.7 %copy.44 = bf16[16,8,128,128]{3,1,2,0:T(8,128)(2,1)} copy(bf16[16,8,128,128]{3,2,1,0:T(8,128)(2,1)} %bitcast.108) | data formatting | bytes 8388608
  27.0 47.3 %all-gather.2.cloned.1.call-done = bf16[32,128,128]{2,1,0:T(8,128)(2,1)} async-done(((bf16[4,128,128]{2,1,0:T(8,128)(2,1)}), bf16[32,128,128]{2,1,0:T(8,128)(2,1)}) %all-gather.2.cloned.1.call-update) | async-done | bytes 1048592 | tf_op jit(solution)/shard_map/all_gather | solution.py:20
  77.2 210.3 %while.10 = (s32[]{:T(128)}, f32[16,128,128]{2,1,0:T(8,128)}, s32[16,48]{1,0:T(8,128)}, bf16[128,16384]{1,0:T(8,128)(2,1)}, s32[16,48]{1,0:T(8,128)}, /*index=5*...) while((s32[]{:T(128)}, f32[16,128,128]{2,1,0:T(8,128)}, s32[16,48]{1,0:T(8,128)}, ...), condition=%wide.region_3.4_spmd, body=%wide.region_2.3_spmd.sunk | while | flops 858797568 | bytes 45156664 | solution.py:38
  86.7 3.7 fusion.58
  91.1 2.9 fusion.54
  99.8 3.7 fusion.58
  113.0 3.7 fusion.58
  117.3 2.9 fusion.54
  126.1 3.7 fusion.58
  130.5 2.9 fusion.54
  139.3 3.7 fusion.58
  152.4 3.7 fusion.58
  156.8 2.9 fusion.54
  165.6 3.7 fusion.58
  169.9 2.9 fusion.54
  178.7 3.7 fusion.58
  183.1 2.9 fusion.54
  191.9 3.7 fusion.58
  205.0 3.7 fusion.58
  209.4 2.9 fusion.54
  218.1 3.7 fusion.58
  222.5 2.9 fusion.54
  231.3 3.7 fusion.58
  235.7 2.9 fusion.54
  244.4 3.7 fusion.58
  257.6 3.7 fusion.58
  270.7 3.7 fusion.58
  283.9 3.7 fusion.58
  292.2 4.5 %all-to-all-start.1 = ((f32[16,2,128,128]{3,2,1,0:T(8,128)}), f32[16,2,128,128]{3,2,1,0:T(8,128)S(1)}, u32[]{:S(2)}, u32[]{:S(2)}) async-start(f32[16,2,128,128]{3,2,1,0:T(8,128)} %copy.18), calls=%async_computation.1 | async-start | bytes 4194304 | tf_op jit(solution)/shard_map/all_to_all | solution.py:61
  298.2 48.2 %all-to-all-done.1 = f32[16,2,128,128]{3,2,1,0:T(8,128)S(1)} async-done(((f32[16,2,128,128]{3,2,1,0:T(8,128)}), f32[16,2,128,128]{3,2,1,0:T(8,128)S(1)}, u32[]{:S(2)}, u32[]{:S(2)}) %all-to-all-start.1) | async-done | bytes 2097184 | tf_op jit(solution)/shard_map/all_to_all | solution.py:61
  349.4 26.0 %all-reduce.2.cloned.1.call-done = f32[8,128,128]{2,1,0:T(8,128)} async-done(((f32[8,128,128]{2,1,0:T(8,128)}), f32[8,128,128]{2,1,0:T(8,128)}) %all-reduce.2.cloned.1.call-update) | async-done | bytes 524304 | tf_op jit(solution)/shard_map/psum | solution.py:71
  (174 shorter events, 142.3 us)
Async XLA Ops:
  6.5 67.8 %all-gather.2.cloned.1.call-start = ((), (), s32[]{:S(2)}) async-start(), calls=%async_computation.2 | async-start | bytes 1179648 | tf_op jit(solution)/shard_map/all_gather | solution.py:20
  10.3 281.9 %all-to-all-start = ((s32[16,1,2]{2,1,0:T(1,128)}), s32[16,1,2]{2,1,0:T(1,128)S(1)}, u32[]{:S(2)}, u32[]{:S(2)}) async-start(s32[16,1,2]{2,1,0:T(1,128)} %bitcast.8), calls=%async_computation | async-start | bytes 16384 | tf_op jit(solution)/shard_map/all_to_all | solution.py:62
  19.3 7.7 %copy-start.1 = (s32[16,1]{0,1:T(1,128)S(1)}, s32[16,1]{0,1:T(1,128)}, u32[]{:S(2)}) copy-start(s32[16,1]{0,1:T(1,128)} %param.14) | copy-start | bytes 196
  81.2 3.1 copy-start
  94.4 3.1 copy-start
  107.5 3.1 copy-start
  120.7 3.1 copy-start
  133.8 3.1 copy-start
  147.0 3.1 copy-start
  160.1 3.1 copy-start
  173.3 3.1 copy-start
  186.4 3.1 copy-start
  199.6 3.1 copy-start
  212.7 3.1 copy-start
  225.8 3.1 copy-start
  239.0 3.1 copy-start
  252.1 3.1 copy-start
  265.3 3.1 copy-start
  278.4 3.1 copy-start
  292.2 54.3 %all-to-all-start.1 = ((f32[16,2,128,128]{3,2,1,0:T(8,128)}), f32[16,2,128,128]{3,2,1,0:T(8,128)S(1)}, u32[]{:S(2)}, u32[]{:S(2)}) async-start(f32[16,2,128,128]{3,2,1,0:T(8,128)} %copy.18), calls=%async_computation.1 | async-start | bytes 4194304 | tf_op jit(solution)/shard_map/all_to_all | solution.py:61
  296.7 78.7 %all-reduce.2.cloned.1.call-start = ((), (), s32[]{:S(2)}) async-start(), calls=%async_computation.3 | async-start | bytes 1048576 | tf_op jit(solution)/shard_map/psum | solution.py:71
Sparse Core Ops, SparseCore 0:
  10.0 64.2 all-gather.1
  349.6 25.8 all-reduce.1
where the time goes:
time: 386 us; the launch traced here: 384 us
  matrix products  153 us (40%)
  waiting for transfers between devices  122 us (32%)
  local copies, waits for them, and re-layouts  78.2 us (20%)
  starting transfers between devices  13.8 us (4%)
  between operations  13.5 us (3%)
    dot_general x48, matrix products, select_tiles(): jnp.dot(onehot, stack_flat, preferred_element_type=jnp.float32)  90.2 us
    dot_general x16, matrix products, one_slot(): jnp.einsum('dov,dvh->oh', left_tile_blocks, middle_product, preferred_ele...  58.6 us
    all_to_all x1, waiting for transfers between devices, shards(): lax.all_to_all(buffer, 'col', split_axis=0, concat_axis=0, tiled=True)  48.2 us
    all_gather x1, waiting for transfers between devices, shards(): gathered = lax.all_gather(amplitudes, 'row', axis=0, tiled=True)  47.3 us
    while x80, local copies, waits for them, and re-layouts  38.3 us
    psum x1, waiting for transfers between devices, shards(): owned_tiles = lax.psum(owned_tiles, 'layer')  26 us
    eq x32, local copies, waits for them, and re-layouts, select_tiles(): picks[:, None] == jnp.arange(count, dtype=jnp.int32)[None, :]  22.5 us
    unnamed x5, local copies, waits for them, and re-layouts  12.5 us
  transfers between devices with their start and end apart: 4, of which 3 were waited for; matrix products, arithmetic and copies ran while one was open for 59% of the time, Pallas kernels for 0%

commit v1 on v0

--- a/solution.py
+++ b/solution.py
@@ -17,7 +17,9 @@
     columns = lax.axis_size("col")
     slot_count = dest_col.shape[0]
     tile_edge = integrals.shape[1]
-    gathered = lax.all_gather(amplitudes, "row", axis=0, tiled=True)
+    gathered = jnp.concatenate(
+        lax.all_to_all(jnp.stack([amplitudes] * lax.axis_size("row")), "row", 0, 0), axis=0
+    )
     amp_total = gathered.shape[0]
     int_total = integrals.shape[0]
     amp_flat = gathered.reshape(amp_total, tile_edge * tile_edge)

time: 386 us -> 368 us (0.953)
  waiting for transfers between devices: 122 us -> 84.5 us
  starting transfers between devices: 13.8 us -> 33.2 us
    all_gather x1 -> x0, waiting for transfers between devices: 47.3 us -> none  [shards(): gathered = lax.all_gather(amplitudes, 'row', axis=0, tiled=True)]
    all_to_all x0 -> x1, starting transfers between devices: none -> 11.6 us  [shards(): lax.all_to_all(jnp.stack([amplitudes] * lax.axis_size('row')), 'row', 0, 0)]
    all_to_all x0 -> x1, waiting for transfers between devices: none -> 9.43 us  [shards(): lax.all_to_all(jnp.stack([amplitudes] * lax.axis_size('row')), 'row', 0, 0)]
    all_to_all x1, starting transfers between devices: 9.01 us -> 14.4 us  [shards(): lax.all_to_all(labels, 'col', split_axis=0, concat_axis=0, tiled=True)]
  transfers between devices with their start and end apart: 4 -> 4, of which waited for: 3 -> 3; matrix products, arithmetic and copies ran while one was open for 59% -> 62% of each run, Pallas kernels for 0% -> 0%
where the time goes in v1:
time: 368 us; the launch traced here: 365 us
  matrix products  154 us (42%)
  waiting for transfers between devices  84.5 us (23%)
  local copies, waits for them, and re-layouts  79.2 us (22%)
  starting transfers between devices  33.2 us (9%)
  between operations  13.5 us (4%)
    dot_general x48, matrix products, select_tiles(): jnp.dot(onehot, stack_flat, preferred_element_type=jnp.float32)  90.2 us
    dot_general x16, matrix products, one_slot(): jnp.einsum('dov,dvh->oh', left_tile_blocks, middle_product, preferred_ele...  58.6 us
    all_to_all x1, waiting for transfers between devices, shards(): lax.all_to_all(buffer, 'col', split_axis=0, concat_axis=0, tiled=True)  48.2 us
    while x80, local copies, waits for them, and re-layouts  38.4 us
    psum x1, waiting for transfers between devices, shards(): owned_tiles = lax.psum(owned_tiles, 'layer')  26.8 us
    eq x32, local copies, waits for them, and re-layouts, select_tiles(): picks[:, None] == jnp.arange(count, dtype=jnp.int32)[None, :]  22.5 us
    all_to_all x1, starting transfers between devices, shards(): lax.all_to_all(labels, 'col', split_axis=0, concat_axis=0, tiled=True)  14.4 us
    all_to_all x1, starting transfers between devices, shards(): lax.all_to_all(jnp.stack([amplitudes] * lax.axis_size('row')), 'row', 0, 0)  11.6 us
  transfers between devices with their start and end apart: 4, of which 3 were waited for; matrix products, arithmetic and copies ran while one was open for 62% of the time, Pallas kernels for 0%

profile of v1, /device:TPU:1, one launch (start us, length us, event | category | flops | bytes accessed | tf_op | source)
XLA Modules:
  0.0 365.5 jit_solution(6332856486099347441)
XLA Ops:
  8.7 11.6 %all-to-all-start.1 = ((bf16[8,4,128,128]{3,2,1,0:T(8,128)(2,1)}), bf16[8,4,128,128]{3,2,1,0:T(8,128)(2,1)S(1)}, u32[]{:S(2)}, u32[]{:S(2)}) async-start(bf16[8,4,128,128]{3,2,1,0:T(8,128)(2,1)} %stack.2), calls=%async_computation.1 | async-start | bytes 2097152 | tf_op jit(solution)/shard_map/all_to_all | solution.py:21
  20.3 7.7 %copy.44 = bf16[16,8,128,128]{3,1,2,0:T(8,128)(2,1)} copy(bf16[16,8,128,128]{3,2,1,0:T(8,128)(2,1)} %bitcast.109) | data formatting | bytes 8388608
  29.6 9.4 %all-to-all-done.1 = bf16[8,4,128,128]{3,2,1,0:T(8,128)(2,1)S(1)} async-done(((bf16[8,4,128,128]{3,2,1,0:T(8,128)(2,1)}), bf16[8,4,128,128]{3,2,1,0:T(8,128)(2,1)S(1)}, u32[]{:S(2)}, u32[]{:S(2)}) %all-to-all-start.1) | async-done | bytes 1048608 | tf_op jit(solution)/shard_map/all_to_all | solution.py:21
  39.1 14.4 %all-to-all-start = ((s32[16,1,2]{2,1,0:T(1,128)}), s32[16,1,2]{2,1,0:T(1,128)S(1)}, u32[]{:S(2)}, u32[]{:S(2)}) async-start(s32[16,1,2]{2,1,0:T(1,128)} %bitcast.8), calls=%async_computation | async-start | bytes 16384 | tf_op jit(solution)/shard_map/all_to_all | solution.py:64
  55.1 210.5 %while.10 = (s32[]{:T(128)}, f32[16,128,128]{2,1,0:T(8,128)}, s32[16,48]{1,0:T(8,128)}, bf16[128,16384]{1,0:T(8,128)(2,1)}, s32[16,48]{1,0:T(8,128)}, /*index=5*...) while((s32[]{:T(128)}, f32[16,128,128]{2,1,0:T(8,128)}, s32[16,48]{1,0:T(8,128)}, ...), condition=%wide.region_3.4_spmd, body=%wide.region_2.3_spmd.sunk | while | flops 858797568 | bytes 45156664 | solution.py:40
  64.6 3.7 %fusion.58 = f32[16,128,128]{2,1,0:T(8,128)} fusion(f32[16,128,128]{2,1,0:T(8,128)} %get-tuple-element.115, s32[]{:T(128)} %get-tuple-element.114, bf16[48,128,128]{2,1,0:T(8,128)(2,1)S(1)} %bitcast.105, bf16[48,128,128]{2,1,0:T(8,128)(2,1)S(1)} %bitcast.106, bf16[48,128,128]{2,1,0:T(8,128)(2,1)} %bitcast.107), kind=kOutput, calls=%fused_computation.10.clone.1 | convolution fusion | flops 403439616 | bytes 4784640 | tf_op jit(solution)/shard_map/while/body/eval_jaxpr/dov,dvh->oh/dot_general | solution.py:36
  69.0 2.9 fusion.54
  77.8 3.7 %fusion.58 = f32[16,128,128]{2,1,0:T(8,128)} fusion(f32[16,128,128]{2,1,0:T(8,128)} %get-tuple-element.115, s32[]{:T(128)} %get-tuple-element.114, bf16[48,128,128]{2,1,0:T(8,128)(2,1)S(1)} %bitcast.105, bf16[48,128,128]{2,1,0:T(8,128)(2,1)S(1)} %bitcast.106, bf16[48,128,128]{2,1,0:T(8,128)(2,1)} %bitcast.107), kind=kOutput, calls=%fused_computation.10.clone.1 | convolution fusion | flops 403439616 | bytes 4784640 | tf_op jit(solution)/shard_map/while/body/eval_jaxpr/dov,dvh->oh/dot_general | solution.py:36
  82.2 2.9 fusion.54
  90.9 3.7 %fusion.58 = f32[16,128,128]{2,1,0:T(8,128)} fusion(f32[16,128,128]{2,1,0:T(8,128)} %get-tuple-element.115, s32[]{:T(128)} %get-tuple-element.114, bf16[48,128,128]{2,1,0:T(8,128)(2,1)S(1)} %bitcast.105, bf16[48,128,128]{2,1,0:T(8,128)(2,1)S(1)} %bitcast.106, bf16[48,128,128]{2,1,0:T(8,128)(2,1)} %bitcast.107), kind=kOutput, calls=%fused_computation.10.clone.1 | convolution fusion | flops 403439616 | bytes 4784640 | tf_op jit(solution)/shard_map/while/body/eval_jaxpr/dov,dvh->oh/dot_general | solution.py:36
  95.3 2.9 fusion.54
  104.1 3.7 %fusion.58 = f32[16,128,128]{2,1,0:T(8,128)} fusion(f32[16,128,128]{2,1,0:T(8,128)} %get-tuple-element.115, s32[]{:T(128)} %get-tuple-element.114, bf16[48,128,128]{2,1,0:T(8,128)(2,1)S(1)} %bitcast.105, bf16[48,128,128]{2,1,0:T(8,128)(2,1)S(1)} %bitcast.106, bf16[48,128,128]{2,1,0:T(8,128)(2,1)} %bitcast.107), kind=kOutput, calls=%fused_computation.10.clone.1 | convolution fusion | flops 403439616 | bytes 4784640 | tf_op jit(solution)/shard_map/while/body/eval_jaxpr/dov,dvh->oh/dot_general | solution.py:36
  117.2 3.7 %fusion.58 = f32[16,128,128]{2,1,0:T(8,128)} fusion(f32[16,128,128]{2,1,0:T(8,128)} %get-tuple-element.115, s32[]{:T(128)} %get-tuple-element.114, bf16[48,128,128]{2,1,0:T(8,128)(2,1)S(1)} %bitcast.105, bf16[48,128,128]{2,1,0:T(8,128)(2,1)S(1)} %bitcast.106, bf16[48,128,128]{2,1,0:T(8,128)(2,1)} %bitcast.107), kind=kOutput, calls=%fused_computation.10.clone.1 | convolution fusion | flops 403439616 | bytes 4784640 | tf_op jit(solution)/shard_map/while/body/eval_jaxpr/dov,dvh->oh/dot_general | solution.py:36
  121.6 2.9 fusion.54
  130.4 3.7 %fusion.58 = f32[16,128,128]{2,1,0:T(8,128)} fusion(f32[16,128,128]{2,1,0:T(8,128)} %get-tuple-element.115, s32[]{:T(128)} %get-tuple-element.114, bf16[48,128,128]{2,1,0:T(8,128)(2,1)S(1)} %bitcast.105, bf16[48,128,128]{2,1,0:T(8,128)(2,1)S(1)} %bitcast.106, bf16[48,128,128]{2,1,0:T(8,128)(2,1)} %bitcast.107), kind=kOutput, calls=%fused_computation.10.clone.1 | convolution fusion | flops 403439616 | bytes 4784640 | tf_op jit(solution)/shard_map/while/body/eval_jaxpr/dov,dvh->oh/dot_general | solution.py:36
  134.8 2.9 fusion.54
  143.5 3.7 %fusion.58 = f32[16,128,128]{2,1,0:T(8,128)} fusion(f32[16,128,128]{2,1,0:T(8,128)} %get-tuple-element.115, s32[]{:T(128)} %get-tuple-element.114, bf16[48,128,128]{2,1,0:T(8,128)(2,1)S(1)} %bitcast.105, bf16[48,128,128]{2,1,0:T(8,128)(2,1)S(1)} %bitcast.106, bf16[48,128,128]{2,1,0:T(8,128)(2,1)} %bitcast.107), kind=kOutput, calls=%fused_computation.10.clone.1 | convolution fusion | flops 403439616 | bytes 4784640 | tf_op jit(solution)/shard_map/while/body/eval_jaxpr/dov,dvh->oh/dot_general | solution.py:36
  156.7 3.7 %fusion.58 = f32[16,128,128]{2,1,0:T(8,128)} fusion(f32[16,128,128]{2,1,0:T(8,128)} %get-tuple-element.115, s32[]{:T(128)} %get-tuple-element.114, bf16[48,128,128]{2,1,0:T(8,128)(2,1)S(1)} %bitcast.105, bf16[48,128,128]{2,1,0:T(8,128)(2,1)S(1)} %bitcast.106, bf16[48,128,128]{2,1,0:T(8,128)(2,1)} %bitcast.107), kind=kOutput, calls=%fused_computation.10.clone.1 | convolution fusion | flops 403439616 | bytes 4784640 | tf_op jit(solution)/shard_map/while/body/eval_jaxpr/dov,dvh->oh/dot_general | solution.py:36
  169.9 3.7 %fusion.58 = f32[16,128,128]{2,1,0:T(8,128)} fusion(f32[16,128,128]{2,1,0:T(8,128)} %get-tuple-element.115, s32[]{:T(128)} %get-tuple-element.114, bf16[48,128,128]{2,1,0:T(8,128)(2,1)S(1)} %bitcast.105, bf16[48,128,128]{2,1,0:T(8,128)(2,1)S(1)} %bitcast.106, bf16[48,128,128]{2,1,0:T(8,128)(2,1)} %bitcast.107), kind=kOutput, calls=%fused_computation.10.clone.1 | convolution fusion | flops 403439616 | bytes 4784640 | tf_op jit(solution)/shard_map/while/body/eval_jaxpr/dov,dvh->oh/dot_general | solution.py:36
  183.0 3.7 %fusion.58 = f32[16,128,128]{2,1,0:T(8,128)} fusion(f32[16,128,128]{2,1,0:T(8,128)} %get-tuple-element.115, s32[]{:T(128)} %get-tuple-element.114, bf16[48,128,128]{2,1,0:T(8,128)(2,1)S(1)} %bitcast.105, bf16[48,128,128]{2,1,0:T(8,128)(2,1)S(1)} %bitcast.106, bf16[48,128,128]{2,1,0:T(8,128)(2,1)} %bitcast.107), kind=kOutput, calls=%fused_computation.10.clone.1 | convolution fusion | flops 403439616 | bytes 4784640 | tf_op jit(solution)/shard_map/while/body/eval_jaxpr/dov,dvh->oh/dot_general | solution.py:36
  196.2 3.7 %fusion.58 = f32[16,128,128]{2,1,0:T(8,128)} fusion(f32[16,128,128]{2,1,0:T(8,128)} %get-tuple-element.115, s32[]{:T(128)} %get-tuple-element.114, bf16[48,128,128]{2,1,0:T(8,128)(2,1)S(1)} %bitcast.105, bf16[48,128,128]{2,1,0:T(8,128)(2,1)S(1)} %bitcast.106, bf16[48,128,128]{2,1,0:T(8,128)(2,1)} %bitcast.107), kind=kOutput, calls=%fused_computation.10.clone.1 | convolution fusion | flops 403439616 | bytes 4784640 | tf_op jit(solution)/shard_map/while/body/eval_jaxpr/dov,dvh->oh/dot_general | solution.py:36
  200.5 2.9 fusion.54
  209.3 3.7 %fusion.58 = f32[16,128,128]{2,1,0:T(8,128)} fusion(f32[16,128,128]{2,1,0:T(8,128)} %get-tuple-element.115, s32[]{:T(128)} %get-tuple-element.114, bf16[48,128,128]{2,1,0:T(8,128)(2,1)S(1)} %bitcast.105, bf16[48,128,128]{2,1,0:T(8,128)(2,1)S(1)} %bitcast.106, bf16[48,128,128]{2,1,0:T(8,128)(2,1)} %bitcast.107), kind=kOutput, calls=%fused_computation.10.clone.1 | convolution fusion | flops 403439616 | bytes 4784640 | tf_op jit(solution)/shard_map/while/body/eval_jaxpr/dov,dvh->oh/dot_general | solution.py:36
  222.5 3.7 %fusion.58 = f32[16,128,128]{2,1,0:T(8,128)} fusion(f32[16,128,128]{2,1,0:T(8,128)} %get-tuple-element.115, s32[]{:T(128)} %get-tuple-element.114, bf16[48,128,128]{2,1,0:T(8,128)(2,1)S(1)} %bitcast.105, bf16[48,128,128]{2,1,0:T(8,128)(2,1)S(1)} %bitcast.106, bf16[48,128,128]{2,1,0:T(8,128)(2,1)} %bitcast.107), kind=kOutput, calls=%fused_computation.10.clone.1 | convolution fusion | flops 403439616 | bytes 4784640 | tf_op jit(solution)/shard_map/while/body/eval_jaxpr/dov,dvh->oh/dot_general | solution.py:36
  226.8 2.9 fusion.54
  235.6 3.7 %fusion.58 = f32[16,128,128]{2,1,0:T(8,128)} fusion(f32[16,128,128]{2,1,0:T(8,128)} %get-tuple-element.115, s32[]{:T(128)} %get-tuple-element.114, bf16[48,128,128]{2,1,0:T(8,128)(2,1)S(1)} %bitcast.105, bf16[48,128,128]{2,1,0:T(8,128)(2,1)S(1)} %bitcast.106, bf16[48,128,128]{2,1,0:T(8,128)(2,1)} %bitcast.107), kind=kOutput, calls=%fused_computation.10.clone.1 | convolution fusion | flops 403439616 | bytes 4784640 | tf_op jit(solution)/shard_map/while/body/eval_jaxpr/dov,dvh->oh/dot_general | solution.py:36
  248.8 3.7 %fusion.58 = f32[16,128,128]{2,1,0:T(8,128)} fusion(f32[16,128,128]{2,1,0:T(8,128)} %get-tuple-element.115, s32[]{:T(128)} %get-tuple-element.114, bf16[48,128,128]{2,1,0:T(8,128)(2,1)S(1)} %bitcast.105, bf16[48,128,128]{2,1,0:T(8,128)(2,1)S(1)} %bitcast.106, bf16[48,128,128]{2,1,0:T(8,128)(2,1)} %bitcast.107), kind=kOutput, calls=%fused_computation.10.clone.1 | convolution fusion | flops 403439616 | bytes 4784640 | tf_op jit(solution)/shard_map/while/body/eval_jaxpr/dov,dvh->oh/dot_general | solution.py:36
  253.1 2.9 fusion.54
  261.9 3.7 %fusion.58 = f32[16,128,128]{2,1,0:T(8,128)} fusion(f32[16,128,128]{2,1,0:T(8,128)} %get-tuple-element.115, s32[]{:T(128)} %get-tuple-element.114, bf16[48,128,128]{2,1,0:T(8,128)(2,1)S(1)} %bitcast.105, bf16[48,128,128]{2,1,0:T(8,128)(2,1)S(1)} %bitcast.106, bf16[48,128,128]{2,1,0:T(8,128)(2,1)} %bitcast.107), kind=kOutput, calls=%fused_computation.10.clone.1 | convolution fusion | flops 403439616 | bytes 4784640 | tf_op jit(solution)/shard_map/while/body/eval_jaxpr/dov,dvh->oh/dot_general | solution.py:36
  270.3 7.0 %all-to-all-start.2 = ((f32[16,2,128,128]{3,2,1,0:T(8,128)}), f32[16,2,128,128]{3,2,1,0:T(8,128)S(1)}, u32[]{:S(2)}, u32[]{:S(2)}) async-start(f32[16,2,128,128]{3,2,1,0:T(8,128)} %copy.18), calls=%async_computation.2 | async-start | bytes 4194304 | tf_op jit(solution)/shard_map/all_to_all | solution.py:63
  278.7 48.2 %all-to-all-done.2 = f32[16,2,128,128]{3,2,1,0:T(8,128)S(1)} async-done(((f32[16,2,128,128]{3,2,1,0:T(8,128)}), f32[16,2,128,128]{3,2,1,0:T(8,128)S(1)}, u32[]{:S(2)}, u32[]{:S(2)}) %all-to-all-start.2) | async-done | bytes 2097184 | tf_op jit(solution)/shard_map/all_to_all | solution.py:63
  329.9 26.8 %all-reduce.2.cloned.1.call-done = f32[8,128,128]{2,1,0:T(8,128)} async-done(((f32[8,128,128]{2,1,0:T(8,128)}), f32[8,128,128]{2,1,0:T(8,128)}) %all-reduce.2.cloned.1.call-update) | async-done | bytes 524304 | tf_op jit(solution)/shard_map/psum | solution.py:73
  (174 shorter events, 144.1 us)
Async XLA Ops:
  8.7 30.4 %all-to-all-start.1 = ((bf16[8,4,128,128]{3,2,1,0:T(8,128)(2,1)}), bf16[8,4,128,128]{3,2,1,0:T(8,128)(2,1)S(1)}, u32[]{:S(2)}, u32[]{:S(2)}) async-start(bf16[8,4,128,128]{3,2,1,0:T(8,128)(2,1)} %stack.2), calls=%async_computation.1 | async-start | bytes 2097152 | tf_op jit(solution)/shard_map/all_to_all | solution.py:21
  20.3 7.7 %copy-start.1 = (s32[16,1]{0,1:T(1,128)S(1)}, s32[16,1]{0,1:T(1,128)}, u32[]{:S(2)}) copy-start(s32[16,1]{0,1:T(1,128)} %param.14) | copy-start | bytes 196
  39.1 231.2 %all-to-all-start = ((s32[16,1,2]{2,1,0:T(1,128)}), s32[16,1,2]{2,1,0:T(1,128)S(1)}, u32[]{:S(2)}, u32[]{:S(2)}) async-start(s32[16,1,2]{2,1,0:T(1,128)} %bitcast.8), calls=%async_computation | async-start | bytes 16384 | tf_op jit(solution)/shard_map/all_to_all | solution.py:64
  59.2 3.1 copy-start
  72.3 3.1 copy-start
  85.5 3.1 copy-start
  98.6 3.1 copy-start
  111.8 3.1 copy-start
  124.9 3.1 copy-start
  138.1 3.1 copy-start
  151.2 3.1 copy-start
  164.4 3.1 copy-start
  177.6 3.1 copy-start
  190.7 3.1 copy-start
  203.9 3.1 copy-start
  217.0 3.1 copy-start
  230.2 3.1 copy-start
  243.3 3.1 copy-start
  256.5 3.1 copy-start
  270.3 56.7 %all-to-all-start.2 = ((f32[16,2,128,128]{3,2,1,0:T(8,128)}), f32[16,2,128,128]{3,2,1,0:T(8,128)S(1)}, u32[]{:S(2)}, u32[]{:S(2)}) async-start(f32[16,2,128,128]{3,2,1,0:T(8,128)} %copy.18), calls=%async_computation.2 | async-start | bytes 4194304 | tf_op jit(solution)/shard_map/all_to_all | solution.py:63
  277.2 79.5 %all-reduce.2.cloned.1.call-start = ((), (), s32[]{:S(2)}) async-start(), calls=%async_computation.3 | async-start | bytes 1048576 | tf_op jit(solution)/shard_map/psum | solution.py:73
Sparse Core Ops, SparseCore 0:
  330.0 26.6 all-reduce.1
